TPU v7x, 32 devices: a whole 2x2x4 slice. The times are simulated.
32 devices in a mesh: segment: 2 (over core), clip: 4 (over z), tile: 4 (over y, x).
Axes of the slice: x: 2, y: 2, z: 4, core: 2. Of those that a mesh axis runs over, the one named last changes fastest.
Arguments:
- video: bfloat16 [4, 4, 3, 12, 4, 256], P('clip', 'tile'), may hold values from -6 to 6
- cotangent: bfloat16 [4, 4, 3, 12, 4, 256], P('clip', 'tile'), may hold values from -6 to 6
- weights: bfloat16 [2, 27, 256, 256], P('segment'), may hold values from -0.078125 to 0.078125
- neighbours: int32 [4, 4, 2], P('clip', 'tile'), may hold values from 0 to 4, as said below
- rows_used: int32 [4, 4], P('clip', 'tile'), may hold values from 3 to 12, as said below
- cols_used: int32 [4], P('clip'), may hold values from 2 to 4, as said below
Outputs:
- section_out: bfloat16 [2, 4, 4, 3, 12, 4, 256], P('segment', 'clip', 'tile')
- grads: float32 [2, 3, 589824], P('segment', None, ('clip', 'tile'))
Inputs may be any that keep to these rules, and one draw needn't show every extreme that they name: `neighbours`: in each clip the strips of its frames lie on the 4 tiles in an order of their own: entry 0 names the tile of the strip above, entry 1 the tile of the strip below, 4 where there is none; exactly one strip of each clip has none above and one has none below, and the entries chain all 4 strips of a clip top to bottom. `rows_used`: in every clip some strip has 12 rows. `cols_used`: some clip has 4 columns.
All inputs are finite; a program needn't handle non-finite values.
Results may differ from a plain program's by a relative error of at most 0.0054.
Values may be sent and summed in bfloat16 or wider, within the bound.
A program may use at most 576 MiB of HBM per device.

v0:
```python
import jax
import jax.numpy as jnp
from jax import lax
from jax.sharding import PartitionSpec as P


def shifted(block, axis, distance):
    devices = range(lax.axis_size(axis))
    route = [(i - distance, i) for i in devices if i - distance in devices]
    return lax.ppermute(block, axis, route)


def silu_grad(values):
    sigmoid = jax.nn.sigmoid(values)
    return sigmoid * (1.0 + values * (1.0 - sigmoid))


def pad_block(strip_field, upper, bottom, row_count):
    frame_count, height, columns, channels = strip_field.shape
    blank = jnp.zeros((frame_count, 1, columns, channels), strip_field.dtype)
    padded = jnp.concatenate([upper[:, None], strip_field, blank], axis=1)
    padded = lax.dynamic_update_slice_in_dim(padded, bottom[:, None], row_count + 1, axis=1)
    return jnp.pad(padded, ((0, 0), (0, 0), (1, 1), (0, 0)))


def patches(stacked, frame_count, height, columns):
    pieces = []
    for depth_off in range(3):
        for row_off in range(3):
            for col_off in range(3):
                pieces.append(
                    stacked[
                        depth_off : depth_off + frame_count,
                        row_off : row_off + height,
                        col_off : col_off + columns,
                    ]
                )
    return jnp.concatenate(pieces, axis=-1).reshape(frame_count * height * columns, -1)


def every_tap_entries(patch_fwd, weighting, start, count, channels):
    span = 9 * channels
    row_total = min(count // channels + 2, span)
    row_low = jnp.minimum(start // channels, span - row_total)
    columns = jnp.concatenate(
        [
            lax.dynamic_slice_in_dim(patch_fwd, tap * span + row_low, row_total, 1)
            for tap in range(3)
        ],
        axis=1,
    )
    contract = (((0,), (0,)), ((), ()))
    block = lax.dot_general(
        columns, weighting, contract, preferred_element_type=jnp.float32
    ).reshape(3, -1)
    return block.T


def local(video, cotangent, weights, neighbours, rows_used, cols_used):
    window = video[0, 0]
    frame_count, height, columns, channels = window.shape
    tile_count = lax.axis_size("tile")
    section = lax.axis_index("segment")
    row_count = rows_used[0, 0]
    col_count = cols_used[0]
    upper_tile = neighbours[0, 0, 0]
    lower_tile = neighbours[0, 0, 1]
    row_ids = jnp.arange(height, dtype=jnp.int32)
    col_ids = jnp.arange(columns, dtype=jnp.int32)
    inside = (row_ids[:, None] < row_count) & (col_ids[None, :] < col_count)
    inside_mask = inside[None, :, :, None]
    kernel = weights[0]
    forward_mat = kernel.reshape(27 * channels, channels)
    backward_mat = kernel[::-1].transpose(0, 2, 1).reshape(27 * channels, channels)
    front_zero = jnp.zeros((2, height + 2, columns + 2, channels), jnp.bfloat16)

    def halo_block(field):
        leading = field[:, 0]
        trailing = lax.dynamic_index_in_dim(field, row_count - 1, axis=1, keepdims=False)
        both_rows = jnp.stack([leading, trailing], axis=1)
        gathered = lax.all_gather(both_rows[None], "tile", axis=0, tiled=True)
        upper = gathered[jnp.minimum(upper_tile, tile_count - 1), :, 1]
        bottom = gathered[jnp.minimum(lower_tile, tile_count - 1), :, 0]
        upper = jnp.where(upper_tile < tile_count, upper, jnp.zeros_like(upper))
        bottom = jnp.where(lower_tile < tile_count, bottom, jnp.zeros_like(bottom))
        return pad_block(field, upper, bottom, row_count)

    def advance(entry, history):
        count = entry.shape[0]
        activated = jax.nn.silu(entry.astype(jnp.float32)).astype(jnp.bfloat16)
        padded = halo_block(activated)
        stacked = jnp.concatenate([history, padded], axis=0)
        mixed = jnp.dot(
            patches(stacked, count, height, columns),
            forward_mat,
            preferred_element_type=jnp.float32,
        ).reshape(entry.shape)
        result = jnp.where(inside_mask, entry.astype(jnp.float32) + mixed, 0.0).astype(jnp.bfloat16)
        return (result, stacked[-2:], padded)

    source = jnp.where(inside_mask, window, jnp.zeros_like(window))
    is_encoder = section == 0
    first_out, first_hist, first_pad = advance(source, front_zero)
    latent = shifted(first_out, "segment", 1)
    second_out, second_hist, second_pad = advance(latent, front_zero)
    own_out = jnp.where(is_encoder, first_out, second_out)
    own_input = jnp.where(is_encoder, source, latent)
    own_pad = jnp.where(is_encoder, first_pad, second_pad)
    target = jnp.where(inside_mask, cotangent[0, 0], jnp.zeros_like(cotangent[0, 0]))
    patch_fwd = patches(
        jnp.concatenate([front_zero, own_pad], axis=0), frame_count, height, columns
    )
    back_stack = jnp.concatenate([halo_block(target), front_zero], axis=0)
    spread = jnp.dot(
        patches(back_stack, frame_count, height, columns),
        backward_mat,
        preferred_element_type=jnp.float32,
    ).reshape(target.shape)
    own_grad = jnp.where(
        inside_mask,
        target.astype(jnp.float32) + silu_grad(own_input.astype(jnp.float32)) * spread,
        0.0,
    ).astype(jnp.bfloat16)
    returned = shifted(own_grad, "segment", -1)
    weighting = jnp.where(is_encoder, returned, target).reshape(-1, channels)
    flat_rows = 9 * channels * channels // lax.axis_size(("clip", "tile"))
    shares = lax.psum_scatter(
        every_tap_entries(
            patch_fwd,
            weighting,
            jnp.int32(0),
            flat_rows * lax.axis_size(("clip", "tile")),
            channels,
        ),
        ("clip", "tile"),
        scatter_dimension=0,
        tiled=True,
    )
    summed = shares.T
    return (own_out[None, None, None], summed[None])


def solution(mesh):
    in_specs = (
        P("clip", "tile", None, None, None, None),
        P("clip", "tile", None, None, None, None),
        P("segment", None, None, None),
        P("clip", "tile", None),
        P("clip", "tile"),
        P("clip"),
    )
    out_specs = (
        P("segment", "clip", "tile", None, None, None, None),
        P("segment", None, ("clip", "tile")),
    )
    return jax.shard_map(local, mesh=mesh, in_specs=in_specs, out_specs=out_specs, check_vma=False)
```

profile of v0, /device:TPU:0, one launch (start us, length us, event | category | flops | bytes accessed | tf_op | source)
XLA Modules:
  0.0 367.3 jit_solution(6660135488782941422)
XLA Ops:
  7.2 0.0 all-reduce.10.cloned.1.call-start
  7.2 1.3 fusion.28
  12.4 0.1 broadcast_and_fusion
  12.5 1.0 bitcast_select_fusion
  13.5 1.0 fusion.18
  14.6 9.7 %all-gather.2 = bf16[12,2,4,256]{3,2,1,0:T(4,128)(2,1)S(1)} all-gather(bf16[3,2,4,256]{3,2,1,0:T(4,128)(2,1)S(1)} %copy.127), channel_id=4, replica_groups=mesh['segment'=2,'clip'=4,'tile'=4] {'tile'}, dimensions={0}, use_global_device_ids=true | all-gather | bytes 61440 | tf_op jit(solution)/shard_map/all_gather | solution.py:81
  24.4 8.2 %all-gather = bf16[12,2,4,256]{3,2,1,0:T(4,128)(2,1)S(1)} all-gather(bf16[3,2,4,256]{3,2,1,0:T(4,128)(2,1)S(1)} %copy.120), channel_id=2, replica_groups=mesh['segment'=2,'clip'=4,'tile'=4] {'tile'}, dimensions={0}, use_global_device_ids=true | all-gather | bytes 61440 | tf_op jit(solution)/shard_map/all_gather | solution.py:81
  32.7 0.1 pad.29.clone
  32.8 0.1 maximum_maximum_fusion.2
  32.9 0.1 dynamic_update_slice.9
  33.7 1.4 copy-done
  35.0 0.9 fusion.2
  35.9 1.3 collective-permute-start
  37.2 0.1 dynamic_update_slice.11
  37.4 5.7 %copy.130 = bf16[1,27,256,256]{2,3,1,0:T(8,128)(2,1)} copy(bf16[1,27,256,256]{3,2,1,0:T(8,128)(2,1)} %param.8) | data formatting | bytes 7077888 | tf_op args[2]
  43.7 4.2 %rev.3 = bf16[27,256,256]{1,2,0:T(8,128)(2,1)} reverse(bf16[27,256,256]{1,2,0:T(8,128)(2,1)} %bitcast.80), dimensions={0} | reverse | bytes 7077888 | tf_op jit(solution)/shard_map/rev | solution.py:74
  48.0 3.0 fusion.14
  51.0 7.3 %all-gather.1 = bf16[12,2,4,256]{3,2,1,0:T(4,128)(2,1)S(1)} all-gather(bf16[3,2,4,256]{3,2,1,0:T(4,128)(2,1)S(1)} %copy.123), channel_id=3, replica_groups=mesh['segment'=2,'clip'=4,'tile'=4] {'tile'}, dimensions={0}, use_global_device_ids=true | all-gather | bytes 61440 | tf_op jit(solution)/shard_map/all_gather | solution.py:81
  58.3 0.1 maximum_maximum_fusion.1
  58.4 0.1 dynamic_update_slice.10
  59.2 1.5 collective-permute-start.1
  60.7 1.7 collective-permute-done.1
  62.4 4.0 %convolution_bitcast_fusion = f32[6912,256]{1,0:T(8,128)} fusion(bf16[3,12,4,6912]{3,1,2,0:T(8,128)(2,1)S(1)} %constant_dynamic-update-slice_fusion.54, bf16[3,12,4,256]{3,1,2,0:T(8,128)(2,1)S(1)} %collective-permute-done.1, pred[]{:T(512)S(6)} %eq.3, bf16[1,1,3,12,4,256]{5,4,3,2,1,0:T(4,128)(2,1)S(1)} %copy-done.3, pred[12,4]{0,1:T(4,128)(4,1)S(1)} %broadcast_and_fusion), kind=kOutput, calls=%fused_computation | convolution fusion | flops 509681664 | bytes 9216049 | tf_op jit(solution)/shard_map/dot_general | solution.py:53
  66.4 10.6 %reshape.152 = f32[3,589824]{1,0:T(4,128)} reshape(f32[6912,256]{1,0:T(8,128)} %convolution_bitcast_fusion) | data formatting | bytes 14155776 | tf_op jit(solution)/shard_map/reshape | solution.py:55
  77.0 0.6 copy-done.4
  77.6 0.6 dynamic-slice
  79.5 1.4 copy-done.1
  80.9 0.9 fusion.5
  81.8 0.7 copy.131
  82.5 275.6 %all-reduce.10.cloned.1.call-done = f32[589824,3]{0,1:T(4,128)} async-done(((f32[589824,3]{0,1:T(4,128)}), f32[589824,3]{0,1:T(4,128)}) %all-reduce.10.cloned.1.call-update) | async-done | bytes 7077904
  358.1 1.2 dynamic-slice_bitcast_fusion
  359.2 1.2 copy.132
  (139 shorter events, 2.2 us)
Async XLA Ops:
  7.2 350.9 %all-reduce.10.cloned.1.call-start = ((), (), s32[]{:S(2)}) async-start(), calls=%async_computation | async-start | bytes 18874368
  33.0 2.0 copy-start
  33.1 2.0 copy-start.2
  35.9 12.0 %collective-permute-start = (bf16[3,12,4,256]{3,1,2,0:T(8,128)(2,1)S(1)}, bf16[3,12,4,256]{3,1,2,0:T(8,128)(2,1)S(1)}, u32[]{:S(2)}, u32[]{:S(2)}) collective-permute-start(bf16[3,12,4,256]{3,1,2,0:T(8,128)(2,1)S(1)} %fusion.2), channel_id=1, source_target_pairs={{0,16},{1,17},{2,18},{3,19},{4,20},{5,21},{6,22},{7,23},{8,24},{9,... | collective-permute-start | bytes 221192 | tf_op jit(solution)/shard_map/ppermute | solution.py:10
  43.7 4.2 %copy-start.3 = (bf16[1,1,3,12,4,256]{5,4,3,2,1,0:T(4,128)(2,1)S(1)}, bf16[1,1,3,12,4,256]{5,4,3,2,1,0:T(4,128)(2,1)}, u32[]{:S(2)}) copy-start(bf16[1,1,3,12,4,256]{5,4,3,2,1,0:T(4,128)(2,1)} %param.7) | copy-start | bytes 221188
  59.2 3.2 collective-permute-start.1
  77.0 0.7 copy-start.4
  78.9 2.0 copy-start.1
Sparse Core Ops, SparseCore 0:
  77.1 280.8 all-reduce.9
where the time goes:
time: 368 us; the launch traced here: 367 us
  waiting for transfers between devices  277 us (75%)
  local copies, waits for them, and re-layouts  31.2 us (8%)
  blocking collectives  25.2 us (7%)
  between operations  19.7 us (5%)
  matrix products  8.71 us (2%)
    unnamed x2, waiting for transfers between devices  276 us
    all_gather x3, blocking collectives, halo_block(): gathered = lax.all_gather(both_rows[None], 'tile', axis=0, tiled=True)  25.2 us
    unnamed x118, local copies, waits for them, and re-layouts  13.4 us
    reshape x1, local copies, waits for them, and re-layouts, every_tap_entries(): block = lax.dot_general(columns, weighting, contract, preferred_element_t...  10.6 us
  transfers between devices with their start and end apart: 3, of which 2 were waited for; matrix products, arithmetic and copies ran while one was open for 4% of the time, Pallas kernels for 0%

commit v1 on v0

--- a/solution.py
+++ b/solution.py
@@ -2,6 +2,17 @@
 import jax.numpy as jnp
 from jax import lax
 from jax.sharding import PartitionSpec as P
+
+
+def around_the_ring(x, axis, dim):
+    n_dev = lax.axis_size(axis)
+    route = [(i, (i + 1) % n_dev) for i in range(n_dev)]
+    terms = [x]
+    for reach in range(1, n_dev):
+        terms = [lax.ppermute(terms[0], axis, route), *terms]
+    out = jnp.concatenate(terms, axis=dim)
+    offset = (lax.axis_index(axis) + 1) * terms[-1].shape[dim]
+    return jnp.roll(out, offset, axis=dim)
 
 
 def shifted(block, axis, distance):
@@ -78,7 +89,7 @@
         leading = field[:, 0]
         trailing = lax.dynamic_index_in_dim(field, row_count - 1, axis=1, keepdims=False)
         both_rows = jnp.stack([leading, trailing], axis=1)
-        gathered = lax.all_gather(both_rows[None], "tile", axis=0, tiled=True)
+        gathered = around_the_ring(both_rows[None], "tile", 0)
         upper = gathered[jnp.minimum(upper_tile, tile_count - 1), :, 1]
         bottom = gathered[jnp.minimum(lower_tile, tile_count - 1), :, 0]
         upper = jnp.where(upper_tile < tile_count, upper, jnp.zeros_like(upper))

time: 368 us -> 367 us (level)
  blocking collectives: 25.2 us -> 0 us
  waiting for transfers between devices: 277 us -> 292 us
  starting transfers between devices: 2.81 us -> 12.6 us
    all_gather x3 -> x0, blocking collectives: 25.2 us -> none  [halo_block(): gathered = lax.all_gather(both_rows[None], 'tile', axis=0, tiled=True)]
    ppermute x0 -> x9, waiting for transfers between devices: none -> 17.1 us  [around_the_ring(): terms = [lax.ppermute(terms[0], axis, route), *terms]]
    ppermute x0 -> x9, starting transfers between devices: none -> 9.99 us  [around_the_ring(): terms = [lax.ppermute(terms[0], axis, route), *terms]]
    unnamed x118 -> x128, local copies, waits for them, and re-layouts: 13.4 us -> 13.9 us
  transfers between devices with their start and end apart: 3 -> 12, of which waited for: 2 -> 8; matrix products, arithmetic and copies ran while one was open for 4% -> 4% of each run, Pallas kernels for 0% -> 0%
where the time goes in v1:
time: 367 us; the launch traced here: 366 us
  waiting for transfers between devices  292 us (80%)
  local copies, waits for them, and re-layouts  29.8 us (8%)
  between operations  19.7 us (5%)
  starting transfers between devices  12.6 us (3%)
  matrix products  6.74 us (2%)
  other arithmetic  5.49 us (1%)
    unnamed x2, waiting for transfers between devices  275 us
    ppermute x9, waiting for transfers between devices, around_the_ring(): terms = [lax.ppermute(terms[0], axis, route), *terms]  17.1 us
    unnamed x128, local copies, waits for them, and re-layouts  13.9 us
    reshape x1, local copies, waits for them, and re-layouts, every_tap_entries(): block = lax.dot_general(columns, weighting, contract, preferred_element_t...  10.6 us
    ppermute x9, starting transfers between devices, around_the_ring(): terms = [lax.ppermute(terms[0], axis, route), *terms]  9.99 us
  transfers between devices with their start and end apart: 12, of which 8 were waited for; matrix products, arithmetic and copies ran while one was open for 4% of the time, Pallas kernels for 0%

profile of v1, /device:TPU:0, one launch (start us, length us, event | category | flops | bytes accessed | tf_op | source)
XLA Modules:
  0.0 366.3 jit_solution(10151456996076139771)
XLA Ops:
  8.6 1.0 fusion.18
  9.7 3.0 collective-permute-start
  12.7 1.0 bitcast_select_fusion
  14.4 1.5 collective-permute-start.7
  15.9 1.5 collective-permute-start.1
  17.5 1.7 collective-permute-done.7
  19.7 1.0 collective-permute-done.1
  20.7 1.4 collective-permute-start.2
  22.1 1.4 fusion.34
  26.1 4.4 %copy.47 = bf16[1,27,256,256]{2,3,1,0:T(8,128)(2,1)S(1)} copy(bf16[1,27,256,256]{3,2,1,0:T(8,128)(2,1)} %param.10) | data formatting | bytes 7077888 | tf_op args[2]
  30.5 2.1 rev.3
  32.7 1.4 collective-permute-start.9
  34.1 1.0 maximum_maximum_fusion
  35.1 2.5 collective-permute-done.9
  37.5 1.0 maximum_maximum_fusion.4
  38.6 1.1 maximum_maximum_fusion.5
  40.5 1.4 copy-done
  41.9 0.9 fusion.2
  42.8 1.3 collective-permute-start.3
  45.0 1.2 copy-done.2
  46.2 1.0 fusion.14
  47.8 4.1 %collective-permute-done.4 = bf16[1,3,2,4,256]{4,2,3,1,0:T(2,128)(2,1)S(1)} collective-permute-done((bf16[1,3,2,4,256]{4,2,3,1,0:T(2,128)(2,1)S(1)}, bf16[1,3,2,4,256]{4,2,3,1,0:T(2,128)(2,1)S(1)}, u32[]{:S(2)}, u32[]{:S(2)}) %collective-permute-start.4) | collective-permute-done | bytes 12320 | tf_op jit(solution)/shard_map/ppermute | solution.py:12
  51.9 4.6 %collective-permute-done.5 = bf16[1,3,2,4,256]{4,2,3,1,0:T(2,128)(2,1)S(1)} collective-permute-done((bf16[1,3,2,4,256]{4,2,3,1,0:T(2,128)(2,1)S(1)}, bf16[1,3,2,4,256]{4,2,3,1,0:T(2,128)(2,1)S(1)}, u32[]{:S(2)}, u32[]{:S(2)}) %collective-permute-start.5) | collective-permute-done | bytes 12320 | tf_op jit(solution)/shard_map/ppermute | solution.py:12
  56.5 1.3 collective-permute-start.10
  57.8 3.3 collective-permute-done.6
  62.3 4.0 %convolution_bitcast_fusion = f32[6912,256]{1,0:T(8,128)} fusion(bf16[3,12,4,6912]{3,1,2,0:T(8,128)(2,1)S(1)} %constant_dynamic-update-slice_fusion.54, bf16[3,12,4,256]{3,1,2,0:T(8,128)(2,1)S(1)} %collective-permute-done.10, pred[]{:T(512)S(6)} %eq.5, bf16[1,1,3,12,4,256]{5,4,3,2,1,0:T(4,128)(2,1)S(1)} %copy-done.6, pred[12,4]{0,1:T(4,128)(4,1)S(1)} %broadcast_and_fusion), kind=kOutput, calls=%fused_computation | convolution fusion | flops 509681664 | bytes 9216049 | tf_op jit(solution)/shard_map/dot_general | solution.py:64
  66.3 10.6 %reshape.152 = f32[3,589824]{1,0:T(4,128)} reshape(f32[6912,256]{1,0:T(8,128)} %convolution_bitcast_fusion) | data formatting | bytes 14155776 | tf_op jit(solution)/shard_map/reshape | solution.py:66
  79.5 1.4 copy-done.1
  80.9 0.9 fusion.5
  82.5 274.6 %all-reduce.10.cloned.1.call-done = f32[589824,3]{0,1:T(4,128)} async-done(((f32[589824,3]{0,1:T(4,128)}), f32[589824,3]{0,1:T(4,128)}) %all-reduce.10.cloned.1.call-update) | async-done | bytes 7077904
  357.1 1.2 dynamic-slice_bitcast_fusion
  358.2 1.2 copy.49
  (158 shorter events, 6.9 us)
Async XLA Ops:
  7.2 349.9 %all-reduce.10.cloned.1.call-start = ((), (), s32[]{:S(2)}) async-start(), calls=%async_computation | async-start | bytes 18874368
  9.6 16.4 %copy-start.3 = (bf16[3,12,4,256]{3,1,2,0:T(8,128)(2,1)}, bf16[3,12,4,256]{3,1,2,0:T(8,128)(2,1)S(1)}, u32[]{:S(2)}) copy-start(bf16[3,12,4,256]{3,1,2,0:T(8,128)(2,1)S(1)} %fusion.18) | copy-start | bytes 221188
  9.7 6.2 %collective-permute-start = (bf16[1,3,2,4,256]{4,2,3,1,0:T(2,128)(2,1)S(1)}, bf16[1,3,2,4,256]{4,2,3,1,0:T(2,128)(2,1)S(1)}, u32[]{:S(2)}, u32[]{:S(2)}) collective-permute-start(bf16[1,3,2,4,256]{4,2,3,1,0:T(2,128)(2,1)S(1)} %maximum_bitcast_fusion), channel_id=1, source_target_pairs={{0,1},{1,2},{2,3},{3,0},{4,5},{5,6},{6,7},{7,4},{8,9},{9,10},{10,1... | collective-permute-start | bytes 36872 | tf_op jit(solution)/shard_map/ppermute | solution.py:12
  13.7 0.6 copy-start.4
  14.4 1.6 copy-start.7
  14.4 4.8 %collective-permute-start.7 = (bf16[1,3,2,4,256]{4,2,3,1,0:T(2,128)(2,1)S(1)}, bf16[1,3,2,4,256]{4,2,3,1,0:T(2,128)(2,1)}, u32[]{:S(2)}, u32[]{:S(2)}) collective-permute-start(bf16[1,3,2,4,256]{4,2,3,1,0:T(2,128)(2,1)S(1)} %maximum_bitcast_fusion.2), channel_id=1, source_target_pairs={{0,1},{1,2},{2,3},{3,0},{4,5},{5,6},{6,7},{7,4},{8,9},{9,10},{10,1... | collective-permute-start | bytes 36872 | tf_op jit(solution)/shard_map/ppermute | solution.py:12
  15.9 3.2 copy-start.8
  15.9 4.7 %collective-permute-start.1 = (bf16[1,3,2,4,256]{4,2,3,1,0:T(2,128)(2,1)S(1)}, bf16[1,3,2,4,256]{4,2,3,1,0:T(2,128)(2,1)}, u32[]{:S(2)}, u32[]{:S(2)}) collective-permute-start(bf16[1,3,2,4,256]{4,2,3,1,0:T(2,128)(2,1)S(1)} %collective-permute-done), channel_id=1, source_target_pairs={{0,1},{1,2},{2,3},{3,0},{4,5},{5,6},{6,7},{7,4},{8,9},{9,10},{10,1... | collective-permute-start | bytes 36872 | tf_op jit(solution)/shard_map/ppermute | solution.py:12
  19.1 13.6 %collective-permute-start.8 = (bf16[1,3,2,4,256]{4,2,3,1,0:T(2,128)(2,1)}, bf16[1,3,2,4,256]{4,2,3,1,0:T(2,128)(2,1)}, u32[]{:S(2)}, u32[]{:S(2)}) collective-permute-start(bf16[1,3,2,4,256]{4,2,3,1,0:T(2,128)(2,1)} %collective-permute-done.7), channel_id=1, source_target_pairs={{0,1},{1,2},{2,3},{3,0},{4,5},{5,6},{6,7},{7,4},{8,9},{9,10},{10,1... | collective-permute-start | bytes 36872 | tf_op jit(solution)/shard_map/ppermute | solution.py:12
  20.7 13.4 %collective-permute-start.2 = (bf16[1,3,2,4,256]{4,2,3,1,0:T(2,128)(2,1)}, bf16[1,3,2,4,256]{4,2,3,1,0:T(2,128)(2,1)}, u32[]{:S(2)}, u32[]{:S(2)}) collective-permute-start(bf16[1,3,2,4,256]{4,2,3,1,0:T(2,128)(2,1)} %collective-permute-done.1), channel_id=1, source_target_pairs={{0,1},{1,2},{2,3},{3,0},{4,5},{5,6},{6,7},{7,4},{8,9},{9,10},{10,1... | collective-permute-start | bytes 36872 | tf_op jit(solution)/shard_map/ppermute | solution.py:12
  32.7 4.8 %collective-permute-start.9 = (bf16[1,3,2,4,256]{4,2,3,1,0:T(2,128)(2,1)}, bf16[1,3,2,4,256]{4,2,3,1,0:T(2,128)(2,1)S(1)}, u32[]{:S(2)}, u32[]{:S(2)}) collective-permute-start(bf16[1,3,2,4,256]{4,2,3,1,0:T(2,128)(2,1)} %collective-permute-done.8), channel_id=1, source_target_pairs={{0,1},{1,2},{2,3},{3,0},{4,5},{5,6},{6,7},{7,4},{8,9},{9,10},{10,1... | collective-permute-start | bytes 36872 | tf_op jit(solution)/shard_map/ppermute | solution.py:12
  39.9 2.0 copy-start
  39.9 2.0 copy-start.5
  42.8 2.2 collective-permute-start.3
  44.2 2.0 copy-start.2
  44.2 2.0 copy-start.6
  47.2 4.6 %collective-permute-start.4 = (bf16[1,3,2,4,256]{4,2,3,1,0:T(2,128)(2,1)S(1)}, bf16[1,3,2,4,256]{4,2,3,1,0:T(2,128)(2,1)S(1)}, u32[]{:S(2)}, u32[]{:S(2)}) collective-permute-start(bf16[1,3,2,4,256]{4,2,3,1,0:T(2,128)(2,1)S(1)} %maximum_bitcast_fusion.1), channel_id=1, source_target_pairs={{0,1},{1,2},{2,3},{3,0},{4,5},{5,6},{6,7},{7,4},{8,9},{9,10},{10,1... | collective-permute-start | bytes 36872 | tf_op jit(solution)/shard_map/ppermute | solution.py:12
  51.9 4.6 %collective-permute-start.5 = (bf16[1,3,2,4,256]{4,2,3,1,0:T(2,128)(2,1)S(1)}, bf16[1,3,2,4,256]{4,2,3,1,0:T(2,128)(2,1)S(1)}, u32[]{:S(2)}, u32[]{:S(2)}) collective-permute-start(bf16[1,3,2,4,256]{4,2,3,1,0:T(2,128)(2,1)S(1)} %collective-permute-done.4), channel_id=1, source_target_pairs={{0,1},{1,2},{2,3},{3,0},{4,5},{5,6},{6,7},{7,4},{8,9},{9,10},{10,1... | collective-permute-start | bytes 36872 | tf_op jit(solution)/shard_map/ppermute | solution.py:12
  56.5 4.6 %collective-permute-start.6 = (bf16[1,3,2,4,256]{4,2,3,1,0:T(2,128)(2,1)S(1)}, bf16[1,3,2,4,256]{4,2,3,1,0:T(2,128)(2,1)S(1)}, u32[]{:S(2)}, u32[]{:S(2)}) collective-permute-start(bf16[1,3,2,4,256]{4,2,3,1,0:T(2,128)(2,1)S(1)} %collective-permute-done.5), channel_id=1, source_target_pairs={{0,1},{1,2},{2,3},{3,0},{4,5},{5,6},{6,7},{7,4},{8,9},{9,10},{10,1... | collective-permute-start | bytes 36872 | tf_op jit(solution)/shard_map/ppermute | solution.py:12
  56.5 5.8 %collective-permute-start.10 = (bf16[3,12,4,256]{3,1,2,0:T(8,128)(2,1)S(1)}, bf16[3,12,4,256]{3,1,2,0:T(8,128)(2,1)S(1)}, u32[]{:S(2)}, u32[]{:S(2)}) collective-permute-start(bf16[3,12,4,256]{3,1,2,0:T(8,128)(2,1)S(1)} %get-tuple-element.11), channel_id=1, source_target_pairs={{16,0},{17,1},{18,2},{19,3},{20,4},{21,5},{22,6},{23,7},{24,8},{25... | collective-permute-start | bytes 221192 | tf_op jit(solution)/shard_map/ppermute | solution.py:21
  77.0 0.7 copy-start.9
  78.9 2.0 copy-start.1
Sparse Core Ops, SparseCore 0:
  77.1 279.9 all-reduce.9
